TPU v7x, 512 devices: a whole 4x8x8 slice. The times are simulated.
512 devices in a mesh: rot: 32 (over y, x_hi, core), tag: 16 (over z, x_lo).
Axes of the slice: x: 4 (x_hi: 2, x_lo: 2; x = x_hi * 2 + x_lo), y: 8, z: 8, core: 2. Of those that a mesh axis runs over, the one named last changes fastest.
Arguments:
- user_factors: bfloat16 [262144, 512], P(('rot', 'tag')), may hold values from -1.1953125 to 1.1953125
- item_factors: bfloat16 [32768, 512], P('rot'), may hold values from -1.1953125 to 1.1953125
- tag_factors: bfloat16 [8192, 512], P('tag'), may hold values from -1.1953125 to 1.1953125
- rating_tiles: int32 [8192, 2], P(('rot', 'tag')), may hold values from 0 to 7, as said below
- rating_counts: int32 [512], P(('rot', 'tag')), may hold values from 1 to 16, as said below
- ratings: bfloat16 [8192, 128, 128], P(('rot', 'tag')), may hold values from -6 to 6
- tag_tiles: int32 [8192, 2], P(('rot', 'tag')), may hold values from 0 to 7, as said below
- tag_values: bfloat16 [8192, 128, 128], P(('rot', 'tag')), may hold values from -6 to 6
Outputs:
- new_users: bfloat16 [262144, 512], P(('rot', 'tag'))
- rotated_items: bfloat16 [32768, 512], P('rot')
- new_tags: bfloat16 [8192, 512], P('tag')
Inputs may be any that keep to these rules, and one draw needn't show every extreme that they name: `rating_tiles`: each device's 16 slots hold distinct tiles; column 0 is below 4, column 1 below 8. `rating_counts`: uneven over devices; some device has all 16 slots live. `tag_tiles`: each device has exactly 16 distinct tiles; column 0 is below 8, column 1 below 4.
All inputs are finite; a program needn't handle non-finite values.
Results may differ from a plain program's by a relative error of at most 0.0043.
Values may be sent and summed in bfloat16 or wider, within the bound.
No kernel may reach another device: no remote copies, remote signals or barrier semaphores. Data moves between devices by JAX's collectives and lax.ppermute only.
A program may use at most 64 MiB of HBM per device.

v0:
```python
import jax
import jax.numpy as jnp
from jax import lax
from jax.sharding import PartitionSpec as P

TILE = 128


def shifted(block, axis, distance):
    devices = range(lax.axis_size(axis))
    route = [((i - distance) % len(devices), i) for i in devices]
    return lax.ppermute(block, axis, route)


def spread_tiles(index, count, tiles):
    empty = jnp.zeros((count,) + tiles.shape[1:], jnp.float32)
    return empty.at[index].add(tiles)


def on_device(
    user_factors,
    item_factors,
    tag_factors,
    rating_tiles,
    rating_counts,
    ratings,
    tag_tiles,
    tag_values,
):
    user_count = user_factors.shape[0]
    item_count = item_factors.shape[0]
    tag_count = tag_factors.shape[0]
    rank = user_factors.shape[1]
    ublock = user_factors.reshape(user_count // TILE, TILE, rank)
    vblock = item_factors.reshape(item_count // TILE, TILE, rank)
    wblock = tag_factors.reshape(tag_count // TILE, TILE, rank)
    user_tiles = ublock[rating_tiles[:, 0]]
    item_tiles = vblock[rating_tiles[:, 1]]
    predicted = jnp.einsum(
        "sur,sir->sui", user_tiles, item_tiles, preferred_element_type=jnp.float32
    )
    live = (jnp.arange(rating_tiles.shape[0]) < rating_counts[0])[:, None, None]
    rating_err = jnp.where(live, predicted - ratings.astype(jnp.float32), 0.0).astype(jnp.bfloat16)
    user_part = jnp.einsum(
        "sui,sir->sur", rating_err, item_tiles, preferred_element_type=jnp.float32
    )
    item_part = jnp.einsum(
        "sui,sur->sir", rating_err, user_tiles, preferred_element_type=jnp.float32
    )
    item_rows = vblock[tag_tiles[:, 0]]
    tag_rows = wblock[tag_tiles[:, 1]]
    tag_err = (
        jnp.einsum("sir,sjr->sij", item_rows, tag_rows, preferred_element_type=jnp.float32)
        - tag_values.astype(jnp.float32)
    ).astype(jnp.bfloat16)
    item_from_tags = jnp.einsum(
        "sij,sjr->sir", tag_err, tag_rows, preferred_element_type=jnp.float32
    )
    tag_part = jnp.einsum("sij,sir->sjr", tag_err, item_rows, preferred_element_type=jnp.float32)
    user_grad = spread_tiles(rating_tiles[:, 0], user_count // TILE, user_part).reshape(
        user_count, rank
    )
    item_grad = spread_tiles(rating_tiles[:, 1], item_count // TILE, item_part)
    item_grad = item_grad.at[tag_tiles[:, 0]].add(item_from_tags).reshape(item_count, rank)
    tag_grad = spread_tiles(tag_tiles[:, 1], tag_count // TILE, tag_part).reshape(tag_count, rank)
    users32 = user_factors.astype(jnp.float32)
    new_users = (users32 - 0.04 * (user_grad + 0.05 * users32)).astype(jnp.bfloat16)
    total = lax.psum(item_grad, "tag")
    items32 = item_factors.astype(jnp.float32)
    new_items = (items32 - 0.04 * (total + 0.05 * items32)).astype(jnp.bfloat16)
    rotated_items = shifted(new_items, "rot", 1)
    tag_total = lax.psum(tag_grad, "rot")
    tags32 = tag_factors.astype(jnp.float32)
    new_tags = (tags32 - 0.04 * (tag_total + 0.05 * tags32)).astype(jnp.bfloat16)
    return (new_users, rotated_items, new_tags)


def solution(mesh):
    placed = (
        P(("rot", "tag"), None),
        P("rot", None),
        P("tag", None),
        P(("rot", "tag"), None),
        P(("rot", "tag")),
        P(("rot", "tag"), None, None),
        P(("rot", "tag"), None),
        P(("rot", "tag"), None, None),
    )
    return jax.shard_map(
        on_device,
        mesh=mesh,
        in_specs=placed,
        out_specs=(P(("rot", "tag"), None), P("rot", None), P("tag", None)),
        check_vma=False,
    )
```

profile of v0, /device:TPU:1, one launch (start us, length us, event | category | flops | bytes accessed | tf_op | source)
XLA Modules:
  0.0 487.4 jit_solution(15541563892529906015)
XLA Ops:
  7.2 0.0 all-reduce.3.cloned.1.call-start
  7.2 0.8 fusion.13
  8.7 3.2 gather_fusion
  11.8 0.7 gather_fusion.1
  12.5 3.2 fusion.4
  15.7 0.0 copy-start.13
  15.8 2.7 fusion.17
  18.5 0.7 gather_fusion.2
  19.2 3.4 gather_fusion.3
  22.6 2.5 fusion.5
  25.2 2.7 fusion.18
  27.9 0.2 broadcast_in_dim.16
  28.1 6.2 %scatter_fusion.1 = f32[8,128,512]{2,1,0:T(8,128)S(1)} fusion(f32[8,128,512]{2,1,0:T(8,128)S(1)} %broadcast_in_dim.16, s32[16]{0:T(128)S(1)} %get-tuple-element.5, f32[16,128,512]{2,1,0:T(8,128)} %fusion.17), kind=kCustom, calls=%fused_computation.5 | custom fusion | flops 1048576 | bytes 12582976 | tf_op jit(solution)/shard_map/scatter-add | solution.py:17
  34.3 6.2 %scatter_fusion.2 = f32[8,128,512]{2,1,0:T(8,128)S(1)} fusion(f32[8,128,512]{2,1,0:T(8,128)S(1)} %scatter_fusion.1, s32[16]{0:T(128)S(1)} %get-tuple-element.4, f32[16,128,512]{2,1,0:T(8,128)} %fusion.18), kind=kCustom, calls=%fused_computation.6 | custom fusion | flops 1048576 | bytes 12582976 | tf_op jit(solution)/shard_map/scatter-add | solution.py:64
  40.5 1.4 copy-done
  41.9 0.0 all-reduce.3.cloned.1.call-update
  41.9 0.0 all-reduce.5.cloned.1.call-start
  41.9 4.5 fusion.19
  46.4 0.1 broadcast.30.clone.1
  46.5 6.1 %scatter_fusion.3 = f32[4,128,512]{2,1,0:T(8,128)S(1)} fusion(f32[4,128,512]{2,1,0:T(8,128)S(1)} %broadcast.30.clone.1, s32[16]{0:T(128)S(1)} %get-tuple-element.3, f32[16,128,512]{2,1,0:T(8,128)} %fusion.19), kind=kCustom, calls=%fused_computation.7 | custom fusion | flops 1048576 | bytes 12582976 | tf_op jit(solution)/shard_map/scatter-add | solution.py:17
  52.6 1.0 copy-done.1
  53.6 0.0 all-reduce.5.cloned.1.call-update
  53.7 136.4 %all-reduce.3.cloned.1.call-done = f32[1024,512]{1,0:T(8,128)} async-done(((f32[1024,512]{1,0:T(8,128)}), f32[1024,512]{1,0:T(8,128)}) %all-reduce.3.cloned.1.call-update) | async-done | bytes 2097168 | tf_op jit(solution)/shard_map/psum | solution.py:68
  190.1 3.0 fusion.2
  193.1 14.7 %collective-permute-start = (bf16[1024,512]{1,0:T(8,128)(2,1)}, bf16[1024,512]{1,0:T(8,128)(2,1)}, u32[]{:S(2)}, u32[]{:S(2)}) collective-permute-start(bf16[1024,512]{1,0:T(8,128)(2,1)} %fusion.2), channel_id=1, source_target_pairs={{496,0},{0,16},{16,32},{32,48},{48,64},{64,80},{80,96},{96,112},{1... | collective-permute-start | bytes 3145736 | tf_op jit(solution)/shard_map/ppermute | solution.py:12
  207.8 2.6 fusion.16
  210.4 0.1 broadcast.30.clone
  210.6 6.1 %scatter_fusion = f32[4,128,512]{2,1,0:T(8,128)S(1)} fusion(f32[4,128,512]{2,1,0:T(8,128)S(1)} %broadcast.30.clone, s32[16]{0:T(128)S(1)} %get-tuple-element.6, f32[16,128,512]{2,1,0:T(8,128)} %fusion.16), kind=kCustom, calls=%fused_computation.4 | custom fusion | flops 1048576 | bytes 12582976 | tf_op jit(solution)/shard_map/scatter-add | solution.py:17
  216.7 1.0 fusion.8
  217.7 258.3 %all-reduce.5.cloned.1.call-done = f32[512,512]{1,0:T(8,128)} async-done(((f32[512,512]{1,0:T(8,128)}), f32[512,512]{1,0:T(8,128)}) %all-reduce.5.cloned.1.call-update) | async-done | bytes 1048592 | tf_op jit(solution)/shard_map/psum | solution.py:72
  476.0 2.2 fusion.11
  478.3 2.3 copy.23
  (30 shorter events, 0.1 us)
Async XLA Ops:
  7.2 182.9 %all-reduce.3.cloned.1.call-start = ((), (), s32[]{:S(2)}) async-start(), calls=%async_computation | async-start | bytes 4194304 | tf_op jit(solution)/shard_map/psum | solution.py:68
  8.6 3.2 copy-start.2
  12.5 3.2 copy-start.7
  12.5 3.2 copy-start.9
  15.7 2.7 copy-start.11
  15.7 2.7 copy-start.13
  19.2 3.4 copy-start.3
  22.6 2.5 copy-start.4
  25.2 2.7 copy-start.10
  40.5 1.4 copy-start
  41.9 434.2 %all-reduce.5.cloned.1.call-start = ((), (), s32[]{:S(2)}) async-start(), calls=%async_computation.1 | async-start | bytes 2097152 | tf_op jit(solution)/shard_map/psum | solution.py:72
  52.6 1.0 copy-start.1
  53.7 154.1 %copy-start.8 = (bf16[16,128,512]{2,1,0:T(8,128)(2,1)S(1)}, bf16[16,128,512]{2,1,0:T(8,128)(2,1)}, u32[]{:S(2)}) copy-start(bf16[16,128,512]{2,1,0:T(8,128)(2,1)} %copy-done.7) | copy-start | bytes 6291460
  190.1 17.7 %copy-start.12 = (bf16[16,128,128]{2,1,0:T(8,128)(2,1)S(1)}, bf16[16,128,128]{2,1,0:T(8,128)(2,1)}, u32[]{:S(2)}) copy-start(bf16[16,128,128]{2,1,0:T(8,128)(2,1)} %copy-done.11) | copy-start | bytes 1572868
  193.1 285.2 %collective-permute-start = (bf16[1024,512]{1,0:T(8,128)(2,1)}, bf16[1024,512]{1,0:T(8,128)(2,1)}, u32[]{:S(2)}, u32[]{:S(2)}) collective-permute-start(bf16[1024,512]{1,0:T(8,128)(2,1)} %fusion.2), channel_id=1, source_target_pairs={{496,0},{0,16},{16,32},{32,48},{48,64},{64,80},{80,96},{96,112},{1... | collective-permute-start | bytes 3145736 | tf_op jit(solution)/shard_map/ppermute | solution.py:12
  210.5 6.2 %copy-start.5 = (bf16[512,512]{1,0:T(8,128)(2,1)S(1)}, bf16[512,512]{1,0:T(8,128)(2,1)}, u32[]{:S(2)}) copy-start(bf16[512,512]{1,0:T(8,128)(2,1)} %param.8) | copy-start | bytes 1572868
  216.7 259.3 %copy-start.6 = (bf16[512,512]{1,0:T(8,128)(2,1)S(1)}, bf16[512,512]{1,0:T(8,128)(2,1)}, u32[]{:S(2)}) copy-start(bf16[512,512]{1,0:T(8,128)(2,1)} %param.10) | copy-start | bytes 1572868
Sparse Core Ops, SparseCore 0:
  42.0 148.0 all-reduce.2
  193.0 283.0 all-reduce.4
where the time goes:
time: 488 us; the launch traced here: 487 us
  waiting for transfers between devices  395 us (81%)
  other arithmetic  31.6 us (6%)
  matrix products  18.2 us (4%)
  between operations  15 us (3%)
  starting transfers between devices  14.8 us (3%)
  local copies, waits for them, and re-layouts  13.1 us (3%)
    psum x1, waiting for transfers between devices, on_device(): tag_total = lax.psum(tag_grad, 'rot')  258 us
    psum x1, waiting for transfers between devices, on_device(): total = lax.psum(item_grad, 'tag')  136 us
    scatter-add x3, other arithmetic, spread_tiles(): return empty.at[index].add(tiles)  18.4 us
    ppermute x1, starting transfers between devices, shifted(): return lax.ppermute(block, axis, route)  14.7 us
  transfers between devices with their start and end apart: 3, of which 2 were waited for; matrix products, arithmetic and copies ran while one was open for 5% of the time, Pallas kernels for 0%

commit v1 on v0

--- a/solution.py
+++ b/solution.py
@@ -69,7 +69,7 @@
     items32 = item_factors.astype(jnp.float32)
     new_items = (items32 - 0.04 * (total + 0.05 * items32)).astype(jnp.bfloat16)
     rotated_items = shifted(new_items, "rot", 1)
-    tag_total = lax.psum(tag_grad, "rot")
+    tag_total = jnp.sum(lax.all_gather(tag_grad, "rot"), axis=0)
     tags32 = tag_factors.astype(jnp.float32)
     new_tags = (tags32 - 0.04 * (tag_total + 0.05 * tags32)).astype(jnp.bfloat16)
     return (new_users, rotated_items, new_tags)

time: 488 us -> 336 us (0.69)
  waiting for transfers between devices: 395 us -> 228 us
  other arithmetic: 31.6 us -> 42.7 us
    psum x1 -> x0, waiting for transfers between devices: 258 us -> none  [on_device(): tag_total = lax.psum(tag_grad, 'rot')]
    psum x1, waiting for transfers between devices: 136 us -> 226 us  [on_device(): total = lax.psum(item_grad, 'tag')]
    reduce_sum x0 -> x1, other arithmetic: none -> 12.3 us  [on_device(): tag_total = jnp.sum(lax.all_gather(tag_grad, 'rot'), axis=0)]
  transfers between devices with their start and end apart: 3 -> 3, of which waited for: 2 -> 2; matrix products, arithmetic and copies ran while one was open for 5% -> 7% of each run, Pallas kernels for 0% -> 0%
where the time goes in v1:
time: 336 us; the launch traced here: 334 us
  waiting for transfers between devices  228 us (68%)
  other arithmetic  42.7 us (13%)
  matrix products  18.3 us (5%)
  between operations  16.4 us (5%)
  starting transfers between devices  15.9 us (5%)
  local copies, waits for them, and re-layouts  13 us (4%)
    psum x1, waiting for transfers between devices, on_device(): total = lax.psum(item_grad, 'tag')  226 us
    scatter-add x3, other arithmetic, spread_tiles(): return empty.at[index].add(tiles)  18.4 us
    ppermute x1, starting transfers between devices, shifted(): return lax.ppermute(block, axis, route)  15.8 us
    reduce_sum x1, other arithmetic, on_device(): tag_total = jnp.sum(lax.all_gather(tag_grad, 'rot'), axis=0)  12.3 us
  transfers between devices with their start and end apart: 3, of which 2 were waited for; matrix products, arithmetic and copies ran while one was open for 7% of the time, Pallas kernels for 0%

profile of v1, /device:TPU:1, one launch (start us, length us, event | category | flops | bytes accessed | tf_op | source)
XLA Modules:
  0.0 334.3 jit_solution(14610351181636947706)
XLA Ops:
  8.0 0.0 all-reduce.2.cloned.1.call-start
  8.0 0.8 fusion.13
  9.5 3.2 gather_fusion
  12.7 0.7 gather_fusion.1
  13.4 3.2 fusion.4
  16.6 2.7 fusion.17
  19.3 0.7 gather_fusion.2
  20.0 3.4 %gather_fusion.3 = bf16[16,128,512]{2,1,0:T(8,128)(2,1)} fusion(bf16[4,128,512]{2,1,0:T(8,128)(2,1)} %bitcast.34, s32[1024]{0:T(1024)S(1)} %get-tuple-element.9), kind=kCustom, calls=%fused_computation.3 | custom fusion | bytes 4194368 | tf_op jit(solution)/shard_map/gather | solution.py:51
  23.4 2.5 fusion.5
  26.0 2.7 fusion.18
  28.7 0.2 broadcast_in_dim.16
  28.9 6.2 %scatter_fusion.1 = f32[8,128,512]{2,1,0:T(8,128)S(1)} fusion(f32[8,128,512]{2,1,0:T(8,128)S(1)} %broadcast_in_dim.16, s32[16]{0:T(128)S(1)} %get-tuple-element.5, f32[16,128,512]{2,1,0:T(8,128)} %fusion.17), kind=kCustom, calls=%fused_computation.5 | custom fusion | flops 1048576 | bytes 12582976 | tf_op jit(solution)/shard_map/scatter-add | solution.py:17
  35.1 6.2 %scatter_fusion.2 = f32[8,128,512]{2,1,0:T(8,128)S(1)} fusion(f32[8,128,512]{2,1,0:T(8,128)S(1)} %scatter_fusion.1, s32[16]{0:T(128)S(1)} %get-tuple-element.4, f32[16,128,512]{2,1,0:T(8,128)} %fusion.18), kind=kCustom, calls=%fused_computation.6 | custom fusion | flops 1048576 | bytes 12582976 | tf_op jit(solution)/shard_map/scatter-add | solution.py:64
  41.3 1.3 copy-done
  42.6 0.0 all-reduce.2.cloned.1.call-update
  42.7 0.0 all-gather.2.cloned.1.call-start
  42.7 4.5 %fusion.19 = f32[16,128,512]{2,1,0:T(8,128)} fusion(bf16[16,128,128]{2,1,0:T(8,128)(2,1)} %copy-done.10, bf16[16,128,512]{2,1,0:T(8,128)(2,1)} %copy-done.3), kind=kOutput, calls=%fused_computation.44 | convolution fusion | flops 268435456 | bytes 6815744 | tf_op jit(solution)/shard_map/sij,sir->sjr/dot_general | solution.py:59
  47.2 0.1 broadcast.30.clone.1
  47.3 6.1 %scatter_fusion.3 = f32[4,128,512]{2,1,0:T(8,128)S(1)} fusion(f32[4,128,512]{2,1,0:T(8,128)S(1)} %broadcast.30.clone.1, s32[16]{0:T(128)S(1)} %get-tuple-element.3, f32[16,128,512]{2,1,0:T(8,128)} %fusion.19), kind=kCustom, calls=%fused_computation.7 | custom fusion | flops 1048576 | bytes 12582976 | tf_op jit(solution)/shard_map/scatter-add | solution.py:17
  53.4 1.0 copy-done.1
  54.4 0.0 all-gather.2.cloned.1.call-update
  54.4 226.0 %all-reduce.2.cloned.1.call-done = f32[1024,512]{1,0:T(8,128)} async-done(((f32[1024,512]{1,0:T(8,128)}), f32[1024,512]{1,0:T(8,128)}) %all-reduce.2.cloned.1.call-update) | async-done | bytes 2097168 | tf_op jit(solution)/shard_map/psum | solution.py:68
  280.5 3.0 fusion.2
  283.5 15.8 %collective-permute-start = (bf16[1024,512]{1,0:T(8,128)(2,1)}, bf16[1024,512]{1,0:T(8,128)(2,1)}, u32[]{:S(2)}, u32[]{:S(2)}) collective-permute-start(bf16[1024,512]{1,0:T(8,128)(2,1)} %fusion.2), channel_id=1, source_target_pairs={{496,0},{0,16},{16,32},{32,48},{48,64},{64,80},{80,96},{96,112},{1... | collective-permute-start | bytes 3145736 | tf_op jit(solution)/shard_map/ppermute | solution.py:12
  299.3 2.8 fusion.16
  302.1 0.1 broadcast.30.clone
  302.2 6.1 %scatter_fusion = f32[4,128,512]{2,1,0:T(8,128)S(1)} fusion(f32[4,128,512]{2,1,0:T(8,128)S(1)} %broadcast.30.clone, s32[16]{0:T(128)S(1)} %get-tuple-element.6, f32[16,128,512]{2,1,0:T(8,128)} %fusion.16), kind=kCustom, calls=%fused_computation.4 | custom fusion | flops 1048576 | bytes 12582976 | tf_op jit(solution)/shard_map/scatter-add | solution.py:17
  308.4 1.0 fusion.8
  309.4 2.0 collective-permute-done
  311.4 12.3 %reduce_sum.9 = f32[512,512]{1,0:T(8,128)S(1)} reduce(f32[32,512,512]{2,1,0:T(8,128)} %all-gather.2.cloned.1.call-done, f32[]{:T(128)} %constant.6.clone.1), dimensions={0}, to_apply=%region_5.6 | reduce | flops 8126464 | bytes 34603012 | tf_op jit(solution)/shard_map/reduce_sum | solution.py:72
  323.6 1.0 fusion.11
  324.6 2.3 copy.25
  (31 shorter events, 0.1 us)
Async XLA Ops:
  8.0 272.5 %all-reduce.2.cloned.1.call-start = ((), (), s32[]{:S(2)}) async-start(), calls=%async_computation | async-start | bytes 4194304 | tf_op jit(solution)/shard_map/psum | solution.py:68
  9.5 3.2 copy-start.2
  13.3 3.2 copy-start.7
  13.4 3.2 copy-start.9
  16.6 2.7 copy-start.11
  16.6 2.7 copy-start.13
  20.0 3.4 %copy-start.3 = (bf16[16,128,512]{2,1,0:T(8,128)(2,1)}, bf16[16,128,512]{2,1,0:T(8,128)(2,1)S(1)}, u32[]{:S(2)}) copy-start(bf16[16,128,512]{2,1,0:T(8,128)(2,1)S(1)} %gather_fusion.2) | copy-start | bytes 6291460
  23.4 2.5 copy-start.4
  26.0 2.7 copy-start.10
  41.3 1.3 copy-start
  42.7 268.7 %all-gather.2.cloned.1.call-start = ((), (), s32[]{:S(2)}) async-start(), calls=%async_computation.1 | async-start | bytes 34603008 | tf_op jit(solution)/shard_map/all_gather | solution.py:72
  53.4 1.0 copy-start.1
  54.4 244.9 %copy-start.8 = (bf16[16,128,512]{2,1,0:T(8,128)(2,1)S(1)}, bf16[16,128,512]{2,1,0:T(8,128)(2,1)}, u32[]{:S(2)}) copy-start(bf16[16,128,512]{2,1,0:T(8,128)(2,1)} %copy-done.7) | copy-start | bytes 6291460
  280.5 18.9 %copy-start.12 = (bf16[16,128,128]{2,1,0:T(8,128)(2,1)S(1)}, bf16[16,128,128]{2,1,0:T(8,128)(2,1)}, u32[]{:S(2)}) copy-start(bf16[16,128,128]{2,1,0:T(8,128)(2,1)} %copy-done.11) | copy-start | bytes 1572868
  283.5 27.9 %collective-permute-start = (bf16[1024,512]{1,0:T(8,128)(2,1)}, bf16[1024,512]{1,0:T(8,128)(2,1)}, u32[]{:S(2)}, u32[]{:S(2)}) collective-permute-start(bf16[1024,512]{1,0:T(8,128)(2,1)} %fusion.2), channel_id=1, source_target_pairs={{496,0},{0,16},{16,32},{32,48},{48,64},{64,80},{80,96},{96,112},{1... | collective-permute-start | bytes 3145736 | tf_op jit(solution)/shard_map/ppermute | solution.py:12
  302.2 6.1 %copy-start.5 = (bf16[512,512]{1,0:T(8,128)(2,1)S(1)}, bf16[512,512]{1,0:T(8,128)(2,1)}, u32[]{:S(2)}) copy-start(bf16[512,512]{1,0:T(8,128)(2,1)} %param.8) | copy-start | bytes 1572868
  309.4 14.3 %copy-start.6 = (bf16[512,512]{1,0:T(8,128)(2,1)S(1)}, bf16[512,512]{1,0:T(8,128)(2,1)}, u32[]{:S(2)}) copy-start(bf16[512,512]{1,0:T(8,128)(2,1)} %param.10) | copy-start | bytes 1572868
Sparse Core Ops, SparseCore 0:
  42.8 237.6 all-reduce.1
Sparse Core Ops, SparseCore 1:
  54.5 242.7 all-gather.1
